TPU v7x, 32 devices: a whole 2x2x4 slice. The times are simulated.
32 devices in a mesh: dp: 16 (over z, y, core), mp: 2 (over x).
Axes of the slice: x: 2, y: 2, z: 4, core: 2. Of those that a mesh axis runs over, the one named last changes fastest.
Arguments:
- features: bfloat16 [2048, 4608], P('dp'), may hold values from -6 to 6
- proj_in: bfloat16 [4608, 2560], P('dp', 'mp'), may hold values from -0.09375 to 0.09375
- proj_out: bfloat16 [2560, 2560], P('mp'), may hold values from -0.125 to 0.125
- expert_gate: bfloat16 [64, 2560, 1536], P('dp', None, 'mp'), may hold values from -0.125 to 0.125
- expert_up: bfloat16 [64, 2560, 1536], P('dp', None, 'mp'), may hold values from -0.125 to 0.125
- expert_down: bfloat16 [64, 1536, 2560], P('dp', 'mp'), may hold values from -0.15625 to 0.15625
- routes: int32 [2048, 6], P('dp'), may hold values from 0 to 63, all different within a row; in each aligned block of 128 rows (0 to 127, 128 to 255, ...) at most 15 rows name the same one
- gate_weights: float32 [2048, 6], P('dp'), may hold values from 0.1 to 0.6
- cotangent: bfloat16 [2048, 2560], P('dp'), may hold values from -0.09375 to 0.09375
- first_in: float32 [4608, 2560], P('dp', 'mp'), may hold values from -2 to 2
- second_in: float32 [4608, 2560], P('dp', 'mp'), may hold values from 0.02 to 1
- first_out: float32 [2560, 2560], P('mp', 'dp'), may hold values from -2 to 2
- second_out: float32 [2560, 2560], P('mp', 'dp'), may hold values from 0.02 to 1
Outputs:
- moe_out: bfloat16 [2048, 2560], P('dp')
- new_proj_in: bfloat16 [4608, 2560], P('dp', 'mp')
- new_proj_out: bfloat16 [2560, 2560], P('mp', 'dp')
- new_first_in: float32 [4608, 2560], P('dp', 'mp')
- new_second_in: float32 [4608, 2560], P('dp', 'mp')
- new_first_out: float32 [2560, 2560], P('mp', 'dp')
- new_second_out: float32 [2560, 2560], P('mp', 'dp')
Inputs may be any that keep to these rules, and one draw needn't show every extreme that they name: `routes`: each row names 6 different experts. Within the rows of one device (aligned blocks of 128 rows) no expert is named more than 15 times, and in every draw some expert is named exactly 15 times in some block.
All inputs are finite; a program needn't handle non-finite values.
Results may differ from a plain program's by a relative error of at most 0.01.
Values may be sent and summed in bfloat16 or wider, within the bound.
A program may use at most 192 MiB of HBM per device.

v0:
```python
import jax
import jax.numpy as jnp
from jax import lax
from jax.sharding import PartitionSpec as P

EXPERTS = 64
TOP = 6
CAP = 15
BETA_ONE = 0.9
BETA_TWO = 0.999
EPSILON = 1e-08
LEARN_RATE = 0.001
WEIGHT_DECAY = 0.1
FIRST_FIX = 1.0 - 0.9**50 * 0.9**50
SECOND_FIX = 1.0 - 0.999**50 * 0.999**50


def gelu_parts(preact):

    def smooth(values):
        return jax.nn.gelu(values, approximate=True)

    result, pullback = jax.vjp(smooth, preact)
    return (result, pullback(jnp.ones_like(preact))[0])


def slot_table(chosen_block):
    chosen = chosen_block.reshape(-1)
    onehot = (chosen[:, None] == jnp.arange(EXPERTS, dtype=jnp.int32)[None, :]).astype(jnp.int32)
    earlier = jnp.cumsum(onehot, axis=0) - onehot
    return (chosen, jnp.sum(earlier * onehot, axis=1))


def adamw_update(weight, gradient, first, second):
    first_new = BETA_ONE * first + (1.0 - BETA_ONE) * gradient
    second_new = BETA_TWO * second + (1.0 - BETA_TWO) * gradient * gradient
    update = first_new / FIRST_FIX / (jnp.sqrt(second_new / SECOND_FIX) + EPSILON)
    current = weight.astype(jnp.float32)
    return (
        (current - LEARN_RATE * (update + WEIGHT_DECAY * current)).astype(jnp.bfloat16),
        first_new,
        second_new,
    )


def expert_pass(inputs, grads_in, w_gate, w_up, w_down):
    gate_projection = jnp.einsum("erd,edf->erf", inputs, w_gate, preferred_element_type=jnp.float32)
    up_projection = jnp.einsum("erd,edf->erf", inputs, w_up, preferred_element_type=jnp.float32)
    sigmoid_gate = jax.nn.sigmoid(gate_projection)
    silu_gate = gate_projection * sigmoid_gate
    inner_activation = (silu_gate * up_projection).astype(jnp.bfloat16)
    out_part = jnp.einsum(
        "erf,efd->erd", inner_activation, w_down, preferred_element_type=jnp.float32
    ).astype(jnp.bfloat16)
    down_weight_gradient = jnp.einsum(
        "erd,efd->erf", grads_in, w_down, preferred_element_type=jnp.float32
    )
    gate_weight_gradient = (
        down_weight_gradient
        * up_projection
        * sigmoid_gate
        * (1.0 + gate_projection * (1.0 - sigmoid_gate))
    ).astype(jnp.bfloat16)
    up_weight_gradient = (down_weight_gradient * silu_gate).astype(jnp.bfloat16)
    input_part = (
        jnp.einsum("erf,edf->erd", gate_weight_gradient, w_gate, preferred_element_type=jnp.float32)
        + jnp.einsum("erf,edf->erd", up_weight_gradient, w_up, preferred_element_type=jnp.float32)
    ).astype(jnp.bfloat16)
    return (out_part, input_part)


def slot_sources(position, flat_weights, total_slots):
    pair_count = position.shape[0]
    owner = (
        jnp.zeros((total_slots,), jnp.int32)
        .at[position]
        .set(jnp.arange(pair_count, dtype=jnp.int32) + 1)
    )
    live = owner > 0
    pair_id = jnp.maximum(owner - 1, 0)
    source_row = pair_id // TOP
    slot_weight = jnp.where(live, flat_weights[pair_id], 0.0)
    return (live, source_row, slot_weight)


def fill_inputs(rows, live, source_row):
    return jnp.where(live[:, None], rows[source_row], jnp.zeros((), rows.dtype))


def fill_grads(grads, slot_weight, source_row):
    return (slot_weight[:, None] * grads[source_row].astype(jnp.float32)).astype(jnp.bfloat16)


def collect_rows(buffer, pair_slots, pair_weights):
    flat = buffer.reshape(-1, buffer.shape[-1])
    total = jnp.zeros((pair_slots.shape[0], flat.shape[1]), jnp.float32)
    for choice_index in range(TOP):
        picked = flat[pair_slots[:, choice_index]].astype(jnp.float32)
        if pair_weights is None:
            total = total + picked
        else:
            total = total + pair_weights[:, choice_index : choice_index + 1] * picked
    return total


def embed_columns(columns, column_start, model_width):
    canvas = jnp.zeros((columns.shape[0], model_width), jnp.float32)
    return lax.dynamic_update_slice_in_dim(canvas, columns.astype(jnp.float32), column_start, 1)


def local(
    features,
    proj_in,
    proj_out,
    expert_gate,
    expert_up,
    expert_down,
    routes,
    gate_weights,
    cotangent,
    first_in,
    second_in,
    first_out,
    second_out,
):
    row_count = features.shape[0]
    model_width = cotangent.shape[1]
    data_parts = lax.axis_size("dp")
    model_parts = lax.axis_size("mp")
    data_place = lax.axis_index("dp")
    model_place = lax.axis_index("mp")
    column_width = model_width // model_parts
    column_start = model_place * column_width
    own_experts = expert_gate.shape[0]
    total_slots = own_experts * data_parts * CAP
    expert_rows = data_parts * CAP
    preact = jnp.dot(
        features,
        lax.all_gather(proj_in, "dp", axis=0, tiled=True),
        preferred_element_type=jnp.float32,
    )
    activated, gelu_slope = gelu_parts(preact)
    hidden = activated.astype(jnp.bfloat16)
    partial_value = jnp.dot(hidden, proj_out, preferred_element_type=jnp.float32)
    chosen, slot_index = slot_table(routes)
    position = chosen * CAP + slot_index
    pair_slots = position.reshape(row_count, TOP)
    live, source_row, slot_weight = slot_sources(position, gate_weights.reshape(-1), total_slots)
    cotangent_cols = lax.dynamic_slice_in_dim(cotangent, column_start, column_width, 1)
    mapped_cols = lax.psum_scatter(partial_value, "mp", scatter_dimension=1, tiled=True).astype(
        jnp.bfloat16
    )
    send_rows = fill_inputs(mapped_cols, live, source_row)
    send_grads = fill_grads(cotangent_cols, slot_weight, source_row)
    send_shape = (data_parts, own_experts, CAP, column_width)
    narrow_rows, narrow_grads = (
        lax.all_to_all(
            send_rows.reshape(send_shape), "dp", split_axis=0, concat_axis=2, tiled=True
        ),
        lax.all_to_all(
            send_grads.reshape(send_shape), "dp", split_axis=0, concat_axis=2, tiled=True
        ),
    )
    recv_rows, recv_grads = (
        lax.all_gather(narrow_rows, "mp", axis=3, tiled=True),
        lax.all_gather(narrow_grads, "mp", axis=3, tiled=True),
    )
    out_part, input_part = expert_pass(
        recv_rows.reshape(own_experts, expert_rows, model_width),
        recv_grads.reshape(own_experts, expert_rows, model_width),
        expert_gate,
        expert_up,
        expert_down,
    )
    back_shape = (1, own_experts, expert_rows, model_width)
    back_out, back_in = (
        lax.all_to_all(out_part.reshape(back_shape), "dp", split_axis=2, concat_axis=0, tiled=True),
        lax.all_to_all(
            input_part.reshape(back_shape), "dp", split_axis=2, concat_axis=0, tiled=True
        ),
    )
    out_terms = collect_rows(back_out, pair_slots, gate_weights) + embed_columns(
        mapped_cols, column_start, model_width
    )
    grad_terms_sum = collect_rows(back_in, pair_slots, None) + embed_columns(
        cotangent_cols, column_start, model_width
    )
    total_out, total_in = lax.psum((out_terms, grad_terms_sum), "mp")
    moe_out = total_out.astype(jnp.bfloat16)
    grad_mapped = total_in.astype(jnp.bfloat16)
    grad_hidden = lax.dot_general(
        grad_mapped, proj_out, (((1,), (1,)), ((), ())), preferred_element_type=jnp.float32
    )
    grad_pre = (grad_hidden * gelu_slope).astype(jnp.bfloat16)
    vis_part = features.shape[1] // data_parts
    width_part = model_width // data_parts
    share_rows = vis_part + width_part
    feature_blocks = features.reshape(row_count, data_parts, vis_part)
    mapped_blocks = grad_mapped.reshape(row_count, data_parts, width_part)
    term_in = jnp.einsum(
        "tnv,th->nvh", feature_blocks, grad_pre, preferred_element_type=jnp.float32
    )
    term_out = jnp.einsum("tnd,th->ndh", mapped_blocks, hidden, preferred_element_type=jnp.float32)
    shares = lax.psum_scatter(
        jnp.concatenate([term_in, term_out], axis=1)
        .reshape(share_rows * lax.axis_size("dp"), hidden.shape[1])
        .astype(jnp.bfloat16),
        "dp",
        scatter_dimension=0,
        tiled=True,
    ).astype(jnp.float32)
    grad_in = shares[:vis_part]
    grad_out = shares[vis_part:].T
    own_out = lax.dynamic_slice_in_dim(proj_out, data_place * width_part, width_part, 1)
    new_in, first_in_new, second_in_new = adamw_update(proj_in, grad_in, first_in, second_in)
    new_out, first_out_new, second_out_new = adamw_update(own_out, grad_out, first_out, second_out)
    return (moe_out, new_in, new_out, first_in_new, second_in_new, first_out_new, second_out_new)


def solution(mesh):
    return jax.shard_map(
        local,
        mesh=mesh,
        in_specs=(
            P("dp", None),
            P("dp", "mp"),
            P("mp", None),
            P("dp", None, "mp"),
            P("dp", None, "mp"),
            P("dp", "mp", None),
            P("dp", None),
            P("dp", None),
            P("dp", None),
            P("dp", "mp"),
            P("dp", "mp"),
            P("mp", "dp"),
            P("mp", "dp"),
        ),
        out_specs=(
            P("dp", None),
            P("dp", "mp"),
            P("mp", "dp"),
            P("dp", "mp"),
            P("dp", "mp"),
            P("mp", "dp"),
            P("mp", "dp"),
        ),
        check_vma=False,
    )
```

profile of v0, /device:TPU:0, one launch (start us, length us, event | category | flops | bytes accessed | tf_op | source)
XLA Modules:
  0.0 924.7 jit_solution(17657232542428289778)
XLA Ops:
  7.2 0.7 all-gather.4.cloned.1.call-update
  7.9 100.7 %all-gather.4.cloned.1.call-done = bf16[4608,1280]{1,0:T(8,128)(2,1)} async-done(((bf16[288,1280]{1,0:T(8,128)(2,1)}), bf16[4608,1280]{1,0:T(8,128)(2,1)}) %all-gather.4.cloned.1.call-update) | async-done | bytes 11796496 | tf_op jit(solution)/shard_map/all_gather | solution.py:139
  108.6 6.4 fusion.52
  115.1 5.0 fusion.49
  120.6 1.8 reduce-window.6
  123.4 3.4 scatter_custom_fusion
  126.9 4.3 gather_fusion.7
  131.4 10.4 %reduce-scatter.3.cloned.1.call-done = f32[128,1280]{1,0:T(8,128)} async-done(((f32[128,2560]{1,0:T(8,128)}), f32[128,1280]{1,0:T(8,128)}) %reduce-scatter.3.cloned.1.call-update) | async-done | bytes 655376 | tf_op jit(solution)/shard_map/reduce_scatter | solution.py:150
  141.8 1.1 convert_element_type.112
  142.9 5.5 gather_fusion
  148.4 2.8 gather.48
  151.5 1.3 copy.63
  152.8 60.9 %all_to_all.66 = bf16[16,4,15,1280]{3,1,2,0:T(4,128)(2,1)S(1)} all-to-all(bf16[16,4,15,1280]{3,1,2,0:T(4,128)(2,1)S(1)} %copy.63), channel_id=1, replica_groups=mesh['dp'=16,'mp'=2] {'dp'}, dimensions={0} | all-to-all | bytes 4915200 | tf_op jit(solution)/shard_map/all_to_all | solution.py:157
  213.7 1.8 copy.64
  215.6 4.3 gather_fusion.8
  219.9 3.0 reshape.121
  223.0 3.4 multiply_convert_fusion
  226.4 2.8 copy.68
  229.2 4.9 all-to-all-start.2
  234.1 45.4 %all-gather.6.cloned.1.call-done = bf16[1,4,240,2560]{3,2,1,0:T(8,128)(2,1)} async-done(((bf16[1,4,240,1280]{3,2,1,0:T(8,128)(2,1)}), bf16[1,4,240,2560]{3,2,1,0:T(8,128)(2,1)}) %all-gather.6.cloned.1.call-update) | async-done | bytes 4915216 | tf_op jit(solution)/shard_map/all_gather | solution.py:165
  279.5 12.7 %fusion.3 = f32[4,240,768]{2,1,0:T(8,128)} fusion(bf16[4,2560,768]{2,1,0:T(8,128)(2,1)} %param.17, bf16[1,4,240,2560]{3,2,1,0:T(8,128)(2,1)} %all-gather.6.cloned.1.call-done), kind=kOutput, calls=%fused_computation.25 | convolution fusion | flops 3774873600 | bytes 23592960 | tf_op jit(solution)/shard_map/erd,edf->erf/dot_general | solution.py:48
  292.3 7.6 fusion.5
  299.8 13.6 %fusion.7 = bf16[1,4,240,2560]{3,2,1,0:T(8,128)(2,1)} fusion(bf16[4,768,2560]{2,1,0:T(8,128)(2,1)} %param.18, f32[4,240,768]{2,1,0:T(8,128)} %fusion.3, f32[4,240,768]{2,1,0:T(8,128)S(1)} %fusion.5), kind=kOutput, calls=%fused_computation.29 | convolution fusion | flops 3781754880 | bytes 26542080 | tf_op jit(solution)/shard_map/erf,efd->erd/dot_general | solution.py:52
  313.5 8.4 copy.65
  321.9 5.7 all-to-all-start.1
  328.0 1.8 copy.69
  329.8 65.3 %all-gather.8.cloned.1.call-done = bf16[1,4,240,2560]{3,2,1,0:T(8,128)(2,1)} async-done(((bf16[1,4,240,1280]{3,2,1,0:T(8,128)(2,1)}), bf16[1,4,240,2560]{3,2,1,0:T(8,128)(2,1)}) %all-gather.8.cloned.1.call-update) | async-done | bytes 4915216 | tf_op jit(solution)/shard_map/all_gather | solution.py:166
  395.2 12.8 %fusion.1 = f32[4,240,768]{2,1,0:T(8,128)} fusion(bf16[4,768,2560]{2,1,0:T(8,128)(2,1)} %param.18, bf16[1,4,240,2560]{3,2,1,0:T(8,128)(2,1)} %all-gather.8.cloned.1.call-done), kind=kOutput, calls=%fused_computation.23 | convolution fusion | flops 3774873600 | bytes 23592960 | tf_op jit(solution)/shard_map/erd,efd->erf/dot_general | solution.py:55
  408.0 13.0 %fusion.16 = f32[4,240,2560]{2,1,0:T(8,128)} fusion(bf16[4,2560,768]{2,1,0:T(8,128)(2,1)} %param.16, f32[4,240,768]{2,1,0:T(8,128)} %copy-done.2, f32[4,240,768]{2,1,0:T(8,128)} %fusion.1, f32[4,240,768]{2,1,0:T(8,128)} %fusion.3), kind=kOutput, calls=%fused_computation.47 | convolution fusion | flops 3782246400 | bytes 34406400 | tf_op jit(solution)/shard_map/erf,edf->erd/dot_general | solution.py:66
  420.9 14.6 %fusion.8 = bf16[1,4,240,2560]{3,2,1,0:T(8,128)(2,1)} fusion(f32[4,240,2560]{2,1,0:T(8,128)} %fusion.16, bf16[4,2560,768]{2,1,0:T(8,128)(2,1)} %param.17, f32[4,240,768]{2,1,0:T(8,128)} %fusion.1, f32[4,240,768]{2,1,0:T(8,128)} %copy-done.2), kind=kOutput, calls=%fused_computation.30 | convolution fusion | flops 3784212480 | bytes 36372480 | tf_op jit(solution)/shard_map/erf,edf->erd/dot_general | solution.py:67
  435.5 8.5 copy.70
  444.0 5.8 all-to-all-start.3
  449.9 1.4 copy.72
  451.6 5.9 copy.66
  457.5 7.6 reshape.114
  465.1 4.7 gather_fusion.6
  469.7 4.7 gather_fusion.5
  474.4 65.5 %all-to-all-done.3 = bf16[1,4,240,2560]{3,1,0,2:T(4,128)(2,1)} async-done(((bf16[1,4,240,2560]{3,1,0,2:T(4,128)(2,1)}), bf16[1,4,240,2560]{3,1,0,2:T(4,128)(2,1)}, u32[]{:S(2)}, u32[]{:S(2)}) %all-to-all-start.3) | async-done | bytes 4915232 | tf_op jit(solution)/shard_map/all_to_all | solution.py:178
  539.9 6.0 copy.71
  545.9 7.8 reshape.118
  553.7 5.5 gather_fusion.14
  559.2 5.5 gather_fusion.13
  564.6 5.5 gather_fusion.4
  570.1 5.5 gather_fusion.12
  575.6 5.5 gather_fusion.3
  581.1 5.5 gather_fusion.11
  586.6 5.7 gather_fusion.2
  592.3 5.5 gather_fusion.10
  597.8 5.5 gather_fusion.1
  603.3 5.5 gather_fusion.9
  608.9 2.6 multiply_add_fusion.1
  611.9 0.5 convert_add_fusion
  612.4 0.6 copy-done.16
  613.1 66.1 %all-reduce.2 = (bf16[128,2560]{1,0:T(8,128)(2,1)}, bf16[128,2560]{1,0:T(8,128)(2,1)}) all-reduce(f32[128,2560]{1,0:T(8,128)S(1)} %add_dynamic-update-slice_fusion.1, f32[128,2560]{1,0:T(8,128)S(1)} %add_dynamic-update-slice_fusion), channel_id=1, replica_groups=mesh['dp'=16,'mp'=2] {'mp'}, use_global_device_ids=true, to_apply=%region_5.6 | all-reduce | flops 655360 | bytes 3932160 | tf_op jit(solution)/shard_map/psum | solution.py:188
  679.2 1.4 copy.73
  680.6 5.4 fusion.11
  686.0 4.6 convolution_convert_fusion.1
  690.6 3.6 fusion
  694.2 10.9 %pad_maximum_fusion = bf16[16,448,1280]{2,1,0:T(8,128)(2,1)} fusion(bf16[16,160,1280]{2,1,0:T(8,128)(2,1)} %convolution_convert_fusion.1, bf16[16,288,1280]{2,1,0:T(8,128)(2,1)S(1)} %fusion), kind=kLoop, calls=%fused_computation.16 | loop fusion | flops 36700160 | bytes 36700160 | tf_op jit(solution)/shard_map/concatenate | solution.py:205
  705.2 1.6 constant_dynamic-slice_fusion
  707.1 204.6 %reduce-scatter.5.cloned.1.call-done = bf16[448,1280]{1,0:T(8,128)(2,1)} async-done(((bf16[7168,1280]{1,0:T(8,128)(2,1)}), bf16[448,1280]{1,0:T(8,128)(2,1)}) %reduce-scatter.5.cloned.1.call-update) | async-done | bytes 1146896 | tf_op jit(solution)/shard_map/reduce_scatter | solution.py:204
  911.7 1.5 convert_element_type.140
  913.4 2.6 fusion.14
  916.0 1.7 fusion.20
  (80 shorter events, 3.9 us)
Async XLA Ops:
  7.2 101.4 %all-gather.4.cloned.1.call-start = ((), (), s32[]{:S(2)}) async-start(), calls=%async_computation.6 | async-start | bytes 12533760 | tf_op jit(solution)/shard_map/all_gather | solution.py:139
  7.9 133.9 %reduce-scatter.3.cloned.1.call-start = ((), (), s32[]{:S(2)}) async-start(), calls=%async_computation.7 | async-start | bytes 1966080 | tf_op jit(solution)/shard_map/reduce_scatter | solution.py:150
  115.0 5.1 copy-start.18
  115.0 8.1 copy-start.17
  120.1 159.4 %all-gather.6.cloned.1.call-start = ((), (), s32[]{:S(2)}) async-start(), calls=%async_computation.8 | async-start | bytes 7372800 | tf_op jit(solution)/shard_map/all_gather | solution.py:165
  213.7 1.8 copy-start.15
  229.2 92.7 %all-to-all-start.2 = ((bf16[16,4,15,1280]{3,1,2,0:T(4,128)(2,1)}), bf16[16,4,15,1280]{3,1,2,0:T(4,128)(2,1)S(1)}, u32[]{:S(2)}, u32[]{:S(2)}) async-start(bf16[16,4,15,1280]{3,1,2,0:T(4,128)(2,1)} %copy.68), calls=%async_computation.3 | async-start | bytes 4915200 | tf_op jit(solution)/shard_map/all_to_all | solution.py:160
  279.5 12.8 %copy-start.19 = (bf16[1,4,240,2560]{3,2,1,0:T(8,128)(2,1)S(1)}, bf16[1,4,240,2560]{3,2,1,0:T(8,128)(2,1)}, u32[]{:S(2)}) copy-start(bf16[1,4,240,2560]{3,2,1,0:T(8,128)(2,1)} %all-gather.6.cloned.1.call-done) | copy-start | bytes 14745604
  299.8 13.7 %copy-start.2 = (f32[4,240,768]{2,1,0:T(8,128)}, f32[4,240,768]{2,1,0:T(8,128)S(1)}, u32[]{:S(2)}) copy-start(f32[4,240,768]{2,1,0:T(8,128)S(1)} %fusion.5) | copy-start | bytes 8847364
  321.9 122.1 %all-to-all-start.1 = ((bf16[1,4,240,2560]{3,1,0,2:T(4,128)(2,1)}), bf16[1,4,240,2560]{3,1,0,2:T(4,128)(2,1)}, u32[]{:S(2)}, u32[]{:S(2)}) async-start(bf16[1,4,240,2560]{3,1,0,2:T(4,128)(2,1)} %copy.65), calls=%async_computation.2 | async-start | bytes 9830400 | tf_op jit(solution)/shard_map/all_to_all | solution.py:177
  327.6 67.6 %all-gather.8.cloned.1.call-start = ((), (), s32[]{:S(2)}) async-start(), calls=%async_computation.9 | async-start | bytes 7372800 | tf_op jit(solution)/shard_map/all_gather | solution.py:166
  444.0 5.9 copy-start
  444.0 95.9 %all-to-all-start.3 = ((bf16[1,4,240,2560]{3,1,0,2:T(4,128)(2,1)}), bf16[1,4,240,2560]{3,1,0,2:T(4,128)(2,1)}, u32[]{:S(2)}, u32[]{:S(2)}) async-start(bf16[1,4,240,2560]{3,1,0,2:T(4,128)(2,1)} %copy.70), calls=%async_computation.4 | async-start | bytes 9830400 | tf_op jit(solution)/shard_map/all_to_all | solution.py:178
  449.8 461.9 %reduce-scatter.5.cloned.1.call-start = ((), (), s32[]{:S(2)}) async-start(), calls=%async_computation.10 | async-start | bytes 19496960 | tf_op jit(solution)/shard_map/reduce_scatter | solution.py:204
  608.8 2.7 copy-start.10
  608.8 2.8 copy-start.4
  608.8 2.9 copy-start.5
  608.8 2.9 copy-start.6
  608.8 2.9 copy-start.7
  608.8 2.9 copy-start.8
  608.8 3.0 copy-start.9
  611.9 1.1 copy-start.16
  686.0 4.6 copy-start.1
  705.2 208.1 %copy-start.3 = (bf16[288,1280]{1,0:T(8,128)(2,1)S(1)}, bf16[288,1280]{1,0:T(8,128)(2,1)}, u32[]{:S(2)}) copy-start(bf16[288,1280]{1,0:T(8,128)(2,1)} %param.14) | copy-start | bytes 2211844
  705.2 208.1 %copy-start.11 = (f32[288,1280]{1,0:T(8,128)S(1)}, f32[288,1280]{1,0:T(8,128)}, u32[]{:S(2)}) copy-start(f32[288,1280]{1,0:T(8,128)} %param.22) | copy-start | bytes 4423684
  911.7 1.7 copy-start.12
  913.4 2.6 copy-start.13
  913.4 2.6 copy-start.14
Sparse Core Ops, SparseCore 0:
  10.3 98.3 all-gather.3
  120.2 21.5 reduce-scatter.2
  215.7 63.7 all-gather.5
  329.9 65.1 all-gather.7
  705.3 206.3 reduce-scatter.4
where the time goes:
time: 934 us; the launch traced here: 925 us
  waiting for transfers between devices  493 us (53%)
  local copies, waits for them, and re-layouts  147 us (16%)
  blocking collectives  127 us (14%)
  matrix products  99.3 us (11%)
  other arithmetic  27.3 us (3%)
  starting transfers between devices  17 us (2%)
  between operations  14.7 us (2%)
    reduce_scatter x1, waiting for transfers between devices, local(): lax.psum_scatter(jnp.concatenate([term_in, term_out], axis=1).reshape(sha...  205 us
    all_gather x1, waiting for transfers between devices, local(): lax.all_gather(proj_in, 'dp', axis=0, tiled=True)  101 us
    psum x1, blocking collectives, local(): total_out, total_in = lax.psum((out_terms, grad_terms_sum), 'mp')  66.1 us
    all_to_all x1, waiting for transfers between devices, local(): lax.all_to_all(input_part.reshape(back_shape), 'dp', split_axis=2, concat...  65.5 us
    all_gather x1, waiting for transfers between devices, local(): lax.all_gather(narrow_grads, 'mp', axis=3, tiled=True)  65.3 us
    gather x12, local copies, waits for them, and re-layouts, collect_rows(): picked = flat[pair_slots[:, choice_index]].astype(jnp.float32)  64.4 us
    all_to_all x1, blocking collectives, local(): lax.all_to_all(send_rows.reshape(send_shape), 'dp', split_axis=0, concat_...  60.9 us
    all_gather x1, waiting for transfers between devices, local(): lax.all_gather(narrow_rows, 'mp', axis=3, tiled=True)  45.4 us
  transfers between devices with their start and end apart: 8, of which 6 were waited for; matrix products, arithmetic and copies ran while one was open for 16% of the time, Pallas kernels for 0%

commit v1 on v0

--- a/solution.py
+++ b/solution.py
@@ -163,7 +163,7 @@
     )
     recv_rows, recv_grads = (
         lax.all_gather(narrow_rows, "mp", axis=3, tiled=True),
-        lax.all_gather(narrow_grads, "mp", axis=3, tiled=True),
+        jnp.concatenate(lax.all_gather(narrow_grads, "mp"), axis=3),
     )
     out_part, input_part = expert_pass(
         recv_rows.reshape(own_experts, expert_rows, model_width),

time: 934 us -> 966 us (1.034)
  local copies, waits for them, and re-layouts: 147 us -> 168 us
    another operation x0 -> x1, local copies, waits for them, and re-layouts: none -> 11.6 us  [local(): recv_grads.reshape(own_experts, expert_rows, model_width)]
    reshape x0 -> x1, local copies, waits for them, and re-layouts: none -> 9.68 us  [local(): jnp.concatenate(lax.all_gather(narrow_grads, 'mp'), axis=3)]
  transfers between devices with their start and end apart: 8 -> 8, of which waited for: 6 -> 6; matrix products, arithmetic and copies ran while one was open for 16% -> 17% of each run, Pallas kernels for 0% -> 0%
where the time goes in v1:
time: 966 us; the launch traced here: 956 us
  waiting for transfers between devices  493 us (51%)
  local copies, waits for them, and re-layouts  168 us (17%)
  blocking collectives  127 us (13%)
  matrix products  99.7 us (10%)
  other arithmetic  27.3 us (3%)
  starting transfers between devices  26.5 us (3%)
  between operations  14.7 us (2%)
    reduce_scatter x1, waiting for transfers between devices, local(): lax.psum_scatter(jnp.concatenate([term_in, term_out], axis=1).reshape(sha...  205 us
    all_gather x1, waiting for transfers between devices, local(): lax.all_gather(proj_in, 'dp', axis=0, tiled=True)  101 us
    psum x1, blocking collectives, local(): total_out, total_in = lax.psum((out_terms, grad_terms_sum), 'mp')  66.1 us
    all_to_all x1, waiting for transfers between devices, local(): lax.all_to_all(input_part.reshape(back_shape), 'dp', split_axis=2, concat...  65.5 us
    all_gather x1, waiting for transfers between devices, local(): lax.all_gather(narrow_grads, 'mp')  65.3 us
    gather x12, local copies, waits for them, and re-layouts, collect_rows(): picked = flat[pair_slots[:, choice_index]].astype(jnp.float32)  64.4 us
    all_to_all x1, blocking collectives, local(): lax.all_to_all(send_rows.reshape(send_shape), 'dp', split_axis=0, concat_...  61 us
    all_gather x1, waiting for transfers between devices, local(): lax.all_gather(narrow_rows, 'mp', axis=3, tiled=True)  45.3 us
  transfers between devices with their start and end apart: 8, of which 6 were waited for; matrix products, arithmetic and copies ran while one was open for 17% of the time, Pallas kernels for 0%

profile of v1, /device:TPU:0, one launch (start us, length us, event | category | flops | bytes accessed | tf_op | source)
XLA Modules:
  0.0 955.8 jit_solution(15266181214440915968)
XLA Ops:
  7.9 100.7 %all-gather.4.cloned.1.call-done = bf16[4608,1280]{1,0:T(8,128)(2,1)} async-done(((bf16[288,1280]{1,0:T(8,128)(2,1)}), bf16[4608,1280]{1,0:T(8,128)(2,1)}) %all-gather.4.cloned.1.call-update) | async-done | bytes 11796496 | tf_op jit(solution)/shard_map/all_gather | solution.py:139
  108.6 6.4 fusion.50
  115.1 5.0 fusion.47
  120.6 1.8 reduce-window.6
  123.4 3.4 scatter_custom_fusion
  126.9 4.3 gather_fusion.7
  131.4 10.4 %reduce-scatter.3.cloned.1.call-done = f32[128,1280]{1,0:T(8,128)} async-done(((f32[128,2560]{1,0:T(8,128)}), f32[128,1280]{1,0:T(8,128)}) %reduce-scatter.3.cloned.1.call-update) | async-done | bytes 655376 | tf_op jit(solution)/shard_map/reduce_scatter | solution.py:150
  141.8 1.1 convert_element_type.112
  142.9 5.5 gather_fusion
  148.4 2.8 gather.48
  151.5 1.3 copy.63
  152.8 61.0 %all_to_all.63 = bf16[16,4,15,1280]{3,1,2,0:T(4,128)(2,1)S(1)} all-to-all(bf16[16,4,15,1280]{3,1,2,0:T(4,128)(2,1)S(1)} %copy.63), channel_id=1, replica_groups=mesh['dp'=16,'mp'=2] {'dp'}, dimensions={0} | all-to-all | bytes 4915200 | tf_op jit(solution)/shard_map/all_to_all | solution.py:157
  213.8 1.8 copy.64
  215.6 4.3 gather_fusion.8
  219.9 3.0 reshape.122
  223.1 3.4 multiply_convert_fusion
  226.4 2.8 copy.68
  229.2 5.0 all-to-all-start.2
  234.2 45.3 %all-gather.6.cloned.1.call-done = bf16[1,4,240,2560]{3,2,1,0:T(8,128)(2,1)} async-done(((bf16[1,4,240,1280]{3,2,1,0:T(8,128)(2,1)}), bf16[1,4,240,2560]{3,2,1,0:T(8,128)(2,1)}) %all-gather.6.cloned.1.call-update) | async-done | bytes 4915216 | tf_op jit(solution)/shard_map/all_gather | solution.py:165
  279.5 12.7 %fusion.1 = f32[4,240,768]{2,1,0:T(8,128)} fusion(bf16[4,2560,768]{2,1,0:T(8,128)(2,1)} %param.17, bf16[1,4,240,2560]{3,2,1,0:T(8,128)(2,1)} %all-gather.6.cloned.1.call-done), kind=kOutput, calls=%fused_computation.23 | convolution fusion | flops 3774873600 | bytes 23592960 | tf_op jit(solution)/shard_map/erd,edf->erf/dot_general | solution.py:48
  292.3 7.6 fusion.3
  299.8 13.6 %fusion.5 = bf16[1,4,240,2560]{3,2,1,0:T(8,128)(2,1)} fusion(bf16[4,768,2560]{2,1,0:T(8,128)(2,1)} %param.18, f32[4,240,768]{2,1,0:T(8,128)} %fusion.1, f32[4,240,768]{2,1,0:T(8,128)S(1)} %fusion.3), kind=kOutput, calls=%fused_computation.27 | convolution fusion | flops 3781754880 | bytes 26542080 | tf_op jit(solution)/shard_map/erf,efd->erd/dot_general | solution.py:52
  313.5 8.4 copy.65
  321.9 5.7 all-to-all-start.1
  327.6 9.9 %all-gather.8.cloned.1.call-start = ((), (), s32[]{:S(2)}) async-start(), calls=%async_computation.9 | async-start | bytes 7372800 | tf_op jit(solution)/shard_map/all_gather | solution.py:166
  337.5 1.8 copy.69
  339.2 65.3 %all-gather.8.cloned.1.call-done = bf16[2,1,4,240,1280]{4,3,2,1,0:T(8,128)(2,1)} async-done(((bf16[1,1,4,240,1280]{4,3,2,1,0:T(8,128)(2,1)}), bf16[2,1,4,240,1280]{4,3,2,1,0:T(8,128)(2,1)}) %all-gather.8.cloned.1.call-update) | async-done | bytes 4915216 | tf_op jit(solution)/shard_map/all_gather | solution.py:166
  404.6 9.7 %copy.70 = bf16[1,4,240,2,1280]{4,3,2,1,0:T(2,128)(2,1)} copy(bf16[1,4,240,2,1280]{4,2,1,0,3:T(8,128)(2,1)} %bitcast.98) | data formatting | bytes 9830400 | tf_op jit(solution)/shard_map/reshape | solution.py:166
  414.3 11.6 %reshape_reshape.3 = bf16[4,240,2560]{2,1,0:T(8,128)(2,1)} reshape(bf16[1,4,240,2,1280]{4,3,2,1,0:T(2,128)(2,1)} %copy.70) | data formatting | bytes 9830400 | tf_op jit(solution)/shard_map/reshape;reshape | solution.py:170
  425.9 12.8 %fusion.51 = f32[4,240,768]{2,1,0:T(8,128)} fusion(bf16[4,240,2560]{2,1,0:T(8,128)(2,1)} %reshape_reshape.3, bf16[4,768,2560]{2,1,0:T(8,128)(2,1)} %param.18), kind=kOutput, calls=%fused_computation.128 | convolution fusion | flops 3774873600 | bytes 23592960 | tf_op jit(solution)/shard_map/erd,efd->erf/dot_general | solution.py:55
  438.7 13.0 %fusion.14 = f32[4,240,2560]{2,1,0:T(8,128)} fusion(bf16[4,2560,768]{2,1,0:T(8,128)(2,1)} %param.16, f32[4,240,768]{2,1,0:T(8,128)} %copy-done.2, f32[4,240,768]{2,1,0:T(8,128)} %fusion.51, f32[4,240,768]{2,1,0:T(8,128)} %fusion.1), kind=kOutput, calls=%fused_computation.45 | convolution fusion | flops 3782246400 | bytes 34406400 | tf_op jit(solution)/shard_map/erf,edf->erd/dot_general | solution.py:66
  451.6 15.0 %fusion.6 = bf16[1,4,240,2560]{3,2,1,0:T(8,128)(2,1)} fusion(f32[4,240,2560]{2,1,0:T(8,128)} %fusion.14, bf16[4,2560,768]{2,1,0:T(8,128)(2,1)} %param.17, f32[4,240,768]{2,1,0:T(8,128)} %fusion.51, f32[4,240,768]{2,1,0:T(8,128)} %copy-done.2), kind=kOutput, calls=%fused_computation.28 | convolution fusion | flops 3784212480 | bytes 36372480 | tf_op jit(solution)/shard_map/erf,edf->erd/dot_general | solution.py:67
  466.6 8.5 copy.71
  475.1 5.8 all-to-all-start.3
  481.0 1.4 copy.73
  482.7 5.9 copy.66
  488.6 7.6 reshape.115
  496.2 4.7 gather_fusion.6
  500.8 4.7 gather_fusion.5
  505.5 65.5 %all-to-all-done.3 = bf16[1,4,240,2560]{3,1,0,2:T(4,128)(2,1)} async-done(((bf16[1,4,240,2560]{3,1,0,2:T(4,128)(2,1)}), bf16[1,4,240,2560]{3,1,0,2:T(4,128)(2,1)}, u32[]{:S(2)}, u32[]{:S(2)}) %all-to-all-start.3) | async-done | bytes 4915232 | tf_op jit(solution)/shard_map/all_to_all | solution.py:178
  571.0 6.0 copy.72
  577.0 7.8 reshape.119
  584.8 5.5 gather_fusion.14
  590.3 5.5 gather_fusion.13
  595.7 5.5 gather_fusion.4
  601.2 5.5 gather_fusion.12
  606.7 5.5 gather_fusion.3
  612.2 5.5 gather_fusion.11
  617.7 5.7 gather_fusion.2
  623.4 5.5 gather_fusion.10
  628.9 5.5 gather_fusion.1
  634.4 5.5 gather_fusion.9
  640.0 2.6 multiply_add_fusion.1
  644.2 66.1 %all-reduce.2 = (bf16[128,2560]{1,0:T(8,128)(2,1)}, bf16[128,2560]{1,0:T(8,128)(2,1)}) all-reduce(f32[128,2560]{1,0:T(8,128)S(1)} %add_dynamic-update-slice_fusion.1, f32[128,2560]{1,0:T(8,128)S(1)} %add_dynamic-update-slice_fusion), channel_id=1, replica_groups=mesh['dp'=16,'mp'=2] {'mp'}, use_global_device_ids=true, to_apply=%region_5.6 | all-reduce | flops 655360 | bytes 3932160 | tf_op jit(solution)/shard_map/psum | solution.py:188
  710.3 1.4 copy.74
  711.7 5.4 fusion.9
  717.2 4.6 convolution_convert_fusion.1
  721.7 3.6 fusion
  725.3 10.9 %pad_maximum_fusion = bf16[16,448,1280]{2,1,0:T(8,128)(2,1)} fusion(bf16[16,160,1280]{2,1,0:T(8,128)(2,1)} %convolution_convert_fusion.1, bf16[16,288,1280]{2,1,0:T(8,128)(2,1)S(1)} %fusion), kind=kLoop, calls=%fused_computation.16 | loop fusion | flops 36700160 | bytes 36700160 | tf_op jit(solution)/shard_map/concatenate | solution.py:205
  736.3 1.6 constant_dynamic-slice_fusion
  738.2 204.6 %reduce-scatter.5.cloned.1.call-done = bf16[448,1280]{1,0:T(8,128)(2,1)} async-done(((bf16[7168,1280]{1,0:T(8,128)(2,1)}), bf16[448,1280]{1,0:T(8,128)(2,1)}) %reduce-scatter.5.cloned.1.call-update) | async-done | bytes 1146896 | tf_op jit(solution)/shard_map/reduce_scatter | solution.py:204
  942.8 1.5 convert_element_type.140
  944.5 2.6 fusion.12
  947.2 1.7 fusion.18
  (82 shorter events, 5.2 us)
Async XLA Ops:
  7.2 101.4 %all-gather.4.cloned.1.call-start = ((), (), s32[]{:S(2)}) async-start(), calls=%async_computation.6 | async-start | bytes 12533760 | tf_op jit(solution)/shard_map/all_gather | solution.py:139
  7.9 133.9 %reduce-scatter.3.cloned.1.call-start = ((), (), s32[]{:S(2)}) async-start(), calls=%async_computation.7 | async-start | bytes 1966080 | tf_op jit(solution)/shard_map/reduce_scatter | solution.py:150
  115.0 5.1 copy-start.18
  115.0 8.1 copy-start.17
  120.1 159.4 %all-gather.6.cloned.1.call-start = ((), (), s32[]{:S(2)}) async-start(), calls=%async_computation.8 | async-start | bytes 7372800 | tf_op jit(solution)/shard_map/all_gather | solution.py:165
  213.8 1.8 copy-start.15
  229.2 92.7 %all-to-all-start.2 = ((bf16[16,4,15,1280]{3,1,2,0:T(4,128)(2,1)}), bf16[16,4,15,1280]{3,1,2,0:T(4,128)(2,1)S(1)}, u32[]{:S(2)}, u32[]{:S(2)}) async-start(bf16[16,4,15,1280]{3,1,2,0:T(4,128)(2,1)} %copy.68), calls=%async_computation.3 | async-start | bytes 4915200 | tf_op jit(solution)/shard_map/all_to_all | solution.py:160
  279.5 12.8 %copy-start.19 = (bf16[1,4,240,2560]{3,2,1,0:T(8,128)(2,1)S(1)}, bf16[1,4,240,2560]{3,2,1,0:T(8,128)(2,1)}, u32[]{:S(2)}) copy-start(bf16[1,4,240,2560]{3,2,1,0:T(8,128)(2,1)} %all-gather.6.cloned.1.call-done) | copy-start | bytes 14745604
  299.8 13.7 %copy-start.2 = (f32[4,240,768]{2,1,0:T(8,128)}, f32[4,240,768]{2,1,0:T(8,128)S(1)}, u32[]{:S(2)}) copy-start(f32[4,240,768]{2,1,0:T(8,128)S(1)} %fusion.3) | copy-start | bytes 8847364
  321.9 153.2 %all-to-all-start.1 = ((bf16[1,4,240,2560]{3,1,0,2:T(4,128)(2,1)}), bf16[1,4,240,2560]{3,1,0,2:T(4,128)(2,1)}, u32[]{:S(2)}, u32[]{:S(2)}) async-start(bf16[1,4,240,2560]{3,1,0,2:T(4,128)(2,1)} %copy.65), calls=%async_computation.2 | async-start | bytes 9830400 | tf_op jit(solution)/shard_map/all_to_all | solution.py:177
  327.6 77.0 %all-gather.8.cloned.1.call-start = ((), (), s32[]{:S(2)}) async-start(), calls=%async_computation.9 | async-start | bytes 7372800 | tf_op jit(solution)/shard_map/all_gather | solution.py:166
  475.1 5.9 copy-start
  475.1 95.9 %all-to-all-start.3 = ((bf16[1,4,240,2560]{3,1,0,2:T(4,128)(2,1)}), bf16[1,4,240,2560]{3,1,0,2:T(4,128)(2,1)}, u32[]{:S(2)}, u32[]{:S(2)}) async-start(bf16[1,4,240,2560]{3,1,0,2:T(4,128)(2,1)} %copy.71), calls=%async_computation.4 | async-start | bytes 9830400 | tf_op jit(solution)/shard_map/all_to_all | solution.py:178
  480.9 461.9 %reduce-scatter.5.cloned.1.call-start = ((), (), s32[]{:S(2)}) async-start(), calls=%async_computation.10 | async-start | bytes 19496960 | tf_op jit(solution)/shard_map/reduce_scatter | solution.py:204
  639.9 2.7 copy-start.10
  639.9 2.8 copy-start.4
  639.9 2.9 copy-start.5
  639.9 2.9 copy-start.6
  639.9 2.9 copy-start.7
  639.9 2.9 copy-start.8
  639.9 3.0 copy-start.9
  643.0 1.1 copy-start.16
  717.1 4.6 copy-start.1
  736.3 208.1 %copy-start.3 = (bf16[288,1280]{1,0:T(8,128)(2,1)S(1)}, bf16[288,1280]{1,0:T(8,128)(2,1)}, u32[]{:S(2)}) copy-start(bf16[288,1280]{1,0:T(8,128)(2,1)} %param.14) | copy-start | bytes 2211844
  736.3 208.1 %copy-start.11 = (f32[288,1280]{1,0:T(8,128)S(1)}, f32[288,1280]{1,0:T(8,128)}, u32[]{:S(2)}) copy-start(f32[288,1280]{1,0:T(8,128)} %param.22) | copy-start | bytes 4423684
  942.8 1.7 copy-start.12
  944.5 2.6 copy-start.13
  944.5 2.6 copy-start.14
Sparse Core Ops, SparseCore 0:
  10.3 98.3 all-gather.3
  120.2 21.5 reduce-scatter.2
  215.7 63.7 all-gather.5
  339.4 65.1 all-gather.7
  736.4 206.3 reduce-scatter.4
